TPU v7x, 32 devices: a whole 2x2x4 slice. The times are simulated.
32 devices in a mesh: row: 8 (over y, x, core), col: 4 (over z).
Axes of the slice: x: 2, y: 2, z: 4, core: 2. Of those that a mesh axis runs over, the one named last changes fastest.
Arguments:
- inverse_blocks: float32 [4096, 4096], P('row', 'col'), may hold values from -0.09375 to 0.09375
- panel: bfloat16 [4096, 4096], P('row', 'col'), may hold values from -1.5 to 1.5
- diag_inverse: float32 [512, 4096], P('row', 'col'), may hold values from -6 to 6
- members: int32 [8, 8], replicated, may hold values from 0 to 7, each once within a row
- counts: int32 [8], replicated, may hold values from 1 to 8, as said below
Outputs:
- offdiag: float32 [4096, 4096], P('row', 'col')
- new_diag: float32 [512, 4096], P('row', 'col')
Inputs may be any that keep to these rules, and one draw needn't show every extreme that they name: Each row of members names every ancestor once. `counts`: some supernode lists all 8 ancestors and some lists one.
All inputs are finite; a program needn't handle non-finite values.
Results may differ from a plain program's by a relative error of at most 0.0003.
Values may be sent and summed in bfloat16 or wider, within the bound.
A program may use at most 128 MiB of HBM per device.

v0:
```python
import jax
import jax.numpy as jnp
from jax import lax
from jax.sharding import PartitionSpec as P

B = 512


def body(inverse_blocks, panel, diag_inverse, members, counts):
    rows_dev = panel.shape[0]
    sup_count = panel.shape[1] // B
    row_index = lax.axis_index("row")
    col_index = lax.axis_index("col")
    ancestor = row_index * rows_dev // B
    first_sup = col_index * sup_count
    local_members = lax.dynamic_slice_in_dim(members, first_sup, sup_count, 0)
    local_counts = lax.dynamic_slice_in_dim(counts, first_sup, sup_count, 0)
    slot_index = jnp.arange(members.shape[1], dtype=jnp.int32)
    live_slot = slot_index[None, :] < local_counts[:, None]
    row_mask = jnp.sum(
        jnp.where((local_members == ancestor) & live_slot, 1.0, 0.0).astype(jnp.float32), axis=1
    )
    column_mask = jnp.repeat(row_mask, B)
    masked = panel * column_mask.astype(jnp.bfloat16)[None, :]
    inverse_rows = lax.all_gather(inverse_blocks, "col", axis=1, tiled=True)
    running = jnp.dot(
        inverse_rows,
        lax.all_gather(masked, "row", axis=0, tiled=True).astype(jnp.float32),
        precision=lax.Precision.HIGHEST,
    )
    offdiag = -(running * column_mask[None, :])
    masked_wide = masked.astype(jnp.float32).reshape(rows_dev, sup_count, B)
    offdiag_wide = offdiag.reshape(rows_dev, sup_count, B)
    diag_terms = jnp.einsum(
        "ikc,ikd->ckd", masked_wide, offdiag_wide, precision=lax.Precision.HIGHEST
    )
    summed = lax.psum_scatter(
        diag_terms.reshape(B, sup_count * B), "row", scatter_dimension=0, tiled=True
    )
    return (offdiag, diag_inverse - summed)


def solution(mesh):
    return jax.shard_map(
        body,
        mesh=mesh,
        in_specs=(P("row", "col"), P("row", "col"), P("row", "col"), P(), P()),
        out_specs=(P("row", "col"), P("row", "col")),
        check_vma=False,
    )
```

profile of v0, /device:TPU:0, one launch (start us, length us, event | category | flops | bytes accessed | tf_op | source)
XLA Modules:
  0.0 291.6 jit_solution(4853133798508175931)
XLA Ops:
  7.2 0.0 copy-start.3
  7.2 0.0 copy-start.1
  7.2 0.0 all-gather.5.cloned.1.call-start
  7.2 0.7 all-gather.5.cloned.1.call-update
  7.9 0.0 all-gather.3.cloned.1.call-start
  8.0 0.0 copy-done.3
  8.0 0.1 dynamic_slice.7
  8.1 0.9 fusion.3
  8.9 0.1 broadcast_bitcast_fusion
  9.0 0.0 copy-done.1
  9.0 1.0 broadcast_multiply_fusion
  10.1 0.0 all-gather.3.cloned.1.call-update
  10.1 0.0 copy-start
  10.1 0.0 reduce-scatter.2.cloned.1.call-start
  10.2 151.8 %all-gather.5.cloned.1.call-done = f32[512,4096]{1,0:T(8,128)} async-done(((f32[512,1024]{1,0:T(8,128)}), f32[512,4096]{1,0:T(8,128)}) %all-gather.5.cloned.1.call-update) | async-done | bytes 8388624 | tf_op jit(solution)/shard_map/all_gather | solution.py:25
  162.0 55.1 %all-gather.3.cloned.1.call-done = bf16[4096,1024]{1,0:T(8,128)(2,1)} async-done(((bf16[512,1024]{1,0:T(8,128)(2,1)}), bf16[4096,1024]{1,0:T(8,128)(2,1)}) %all-gather.3.cloned.1.call-update) | async-done | bytes 8388624 | tf_op jit(solution)/shard_map/all_gather | solution.py:28
  217.0 18.9 %multiply_negate_fusion = f32[1024,512]{1,0:T(8,128)S(1)} fusion(bf16[4096,1024]{1,0:T(8,128)(2,1)} %all-gather.3.cloned.1.call-done, f32[512,4096]{1,0:T(8,128)} %all-gather.5.cloned.1.call-done, f32[1024]{0:T(1024)S(1)} %bitcast.21), kind=kOutput, calls=%fused_computation | convolution fusion | flops 25770852352 | bytes 18878464 | tf_op jit(solution)/shard_map/dot_general | solution.py:26
  235.9 0.0 copy-done
  235.9 3.1 %fusion = f32[2,512,512]{2,1,0:T(8,128)} fusion(f32[512,2,512]{0,2,1:T(8,128)S(1)} %bitcast.17, bf16[64,2,8,512]{3,2,1,0:T(8,128)(2,1)S(1)} %bitcast.16), kind=kOutput, calls=%fused_computation.1 | convolution fusion | flops 3221225472 | bytes 5242880 | tf_op jit(solution)/shard_map/ikc,ikd->ckd/dot_general | solution.py:34
  239.0 2.9 %copy.8 = f32[512,1024]{1,0:T(8,128)} copy(f32[512,1024]{0,1:T(8,128)} %bitcast.19) | data formatting | bytes 4194304 | tf_op jit(solution)/shard_map/reshape | solution.py:38
  242.0 0.0 reduce-scatter.2.cloned.1.call-update
  242.0 0.0 copy-start.2
  242.0 1.8 copy.9
  243.8 39.6 %reduce-scatter.2.cloned.1.call-done = f32[64,1024]{1,0:T(8,128)} async-done(((f32[512,1024]{1,0:T(8,128)}), f32[64,1024]{1,0:T(8,128)}) %reduce-scatter.2.cloned.1.call-update) | async-done | bytes 262160 | tf_op jit(solution)/shard_map/reduce_scatter | solution.py:37
  283.4 0.0 copy-done.2
  283.4 1.7 sub.8
  (2 shorter events, 0.0 us)
Async XLA Ops:
  7.2 0.8 copy-start.3
  7.2 1.9 copy-start.1
  7.2 154.8 %all-gather.5.cloned.1.call-start = ((), (), s32[]{:S(2)}) async-start(), calls=%async_computation.2 | async-start | bytes 10485760 | tf_op jit(solution)/shard_map/all_gather | solution.py:25
  7.9 209.1 %all-gather.3.cloned.1.call-start = ((), (), s32[]{:S(2)}) async-start(), calls=%async_computation.1 | async-start | bytes 9437184 | tf_op jit(solution)/shard_map/all_gather | solution.py:28
  10.1 225.8 %copy-start = (bf16[512,1024]{1,0:T(8,128)(2,1)S(1)}, bf16[512,1024]{1,0:T(8,128)(2,1)}, u32[]{:S(2)}) copy-start(bf16[512,1024]{1,0:T(8,128)(2,1)} %broadcast_multiply_fusion) | copy-start | bytes 3145732
  10.1 273.3 %reduce-scatter.2.cloned.1.call-start = ((), (), s32[]{:S(2)}) async-start(), calls=%async_computation.3 | async-start | bytes 2359296 | tf_op jit(solution)/shard_map/reduce_scatter | solution.py:37
  242.0 41.4 %copy-start.2 = (f32[64,1024]{1,0:T(8,128)S(1)}, f32[64,1024]{1,0:T(8,128)}, u32[]{:S(2)}) copy-start(f32[64,1024]{1,0:T(8,128)} %param.7) | copy-start | bytes 786436
Sparse Core Ops, SparseCore 0:
  9.6 152.3 all-gather.4
  164.4 52.5 all-gather.2
  242.1 41.2 reduce-scatter.1
where the time goes:
time: 292 us
  waiting for transfers between devices  247 us (85%)
  matrix products  22 us (8%)
  between operations  13.8 us (5%)
  local copies, waits for them, and re-layouts  4.93 us (2%)
  other arithmetic  3.6 us (1%)
    all_gather x1, waiting for transfers between devices, body(): inverse_rows = lax.all_gather(inverse_blocks, 'col', axis=1, tiled=True)  152 us
    all_gather x1, waiting for transfers between devices, body(): lax.all_gather(masked, 'row', axis=0, tiled=True).astype(jnp.float32)  55.1 us
    reduce_scatter x1, waiting for transfers between devices, body(): lax.psum_scatter(diag_terms.reshape(B, sup_count * B), 'row', scatter_dim...  39.6 us
    dot_general x1, matrix products, body(): jnp.dot(inverse_rows, lax.all_gather(masked, 'row', axis=0, tiled=True).a...  18.9 us
  transfers between devices with their start and end apart: 3, of which 3 were waited for; matrix products, arithmetic and copies ran while one was open for 1% of the time, Pallas kernels for 0%

commit v1 on v0

--- a/solution.py
+++ b/solution.py
@@ -4,6 +4,27 @@
 from jax.sharding import PartitionSpec as P
 
 B = 512
+
+
+def joined_along(pieces, dim):
+    pieces = jnp.moveaxis(pieces, 0, dim)
+    shape = pieces.shape
+    return pieces.reshape(*shape[:dim], shape[dim] * shape[dim + 1], *shape[dim + 2 :])
+
+
+def grow_blocks(array, axis):
+    devices, index = (lax.axis_size(axis), lax.axis_index(axis))
+    tiles, bit = (array[None], 1)
+    while bit < devices:
+        other = lax.ppermute(tiles, axis, [(i, i ^ bit) for i in range(devices)])
+        low = index & bit == 0
+        tiles = jnp.concatenate([jnp.where(low, tiles, other), jnp.where(low, other, tiles)])
+        bit *= 2
+    return tiles
+
+
+def collect(value, axis, dim):
+    return joined_along(grow_blocks(value, axis), dim)
 
 
 def body(inverse_blocks, panel, diag_inverse, members, counts):
@@ -22,7 +43,7 @@
     )
     column_mask = jnp.repeat(row_mask, B)
     masked = panel * column_mask.astype(jnp.bfloat16)[None, :]
-    inverse_rows = lax.all_gather(inverse_blocks, "col", axis=1, tiled=True)
+    inverse_rows = collect(inverse_blocks, "col", 1)
     running = jnp.dot(
         inverse_rows,
         lax.all_gather(masked, "row", axis=0, tiled=True).astype(jnp.float32),

time: 292 us -> 334 us (1.14)
  waiting for transfers between devices: 247 us -> 268 us
  other arithmetic: 3.6 us -> 19.2 us
  starting transfers between devices: 0.12 us -> 5.92 us
    ppermute x0 -> x2, waiting for transfers between devices: none -> 226 us  [grow_blocks(): other = lax.ppermute(tiles, axis, [(i, i ^ bit) for i in range(devices)])]
    all_gather x1 -> x0, waiting for transfers between devices: 152 us -> none  [body(): inverse_rows = lax.all_gather(inverse_blocks, 'col', axis=1, tiled=True)]
    all_gather x1, waiting for transfers between devices: 55.1 us -> 0.01 us  [body(): lax.all_gather(masked, 'row', axis=0, tiled=True).astype(jnp.float32)]
    select_n x0 -> x2, other arithmetic: none -> 7.5 us  [grow_blocks(): jnp.where(low, tiles, other)]
    concatenate x0 -> x2, other arithmetic: none -> 6.86 us  [grow_blocks(): jnp.concatenate([jnp.where(low, tiles, other), jnp.where(low, other, tile...]
    ppermute x0 -> x2, starting transfers between devices: none -> 5.84 us  [grow_blocks(): other = lax.ppermute(tiles, axis, [(i, i ^ bit) for i in range(devices)])]
  transfers between devices with their start and end apart: 3 -> 4, of which waited for: 3 -> 3; matrix products, arithmetic and copies ran while one was open for 1% -> 5% of each run, Pallas kernels for 0% -> 0%
where the time goes in v1:
time: 334 us
  waiting for transfers between devices  268 us (80%)
  matrix products  19.7 us (6%)
  other arithmetic  19.2 us (6%)
  between operations  14.1 us (4%)
  local copies, waits for them, and re-layouts  6.62 us (2%)
  starting transfers between devices  5.92 us (2%)
    ppermute x2, waiting for transfers between devices, grow_blocks(): other = lax.ppermute(tiles, axis, [(i, i ^ bit) for i in range(devices)])  226 us
    reduce_scatter x1, waiting for transfers between devices, body(): lax.psum_scatter(diag_terms.reshape(B, sup_count * B), 'row', scatter_dim...  42.4 us
    dot_general x1, matrix products, body(): jnp.dot(inverse_rows, lax.all_gather(masked, 'row', axis=0, tiled=True).a...  16.3 us
    select_n x2, other arithmetic, grow_blocks(): jnp.where(low, tiles, other)  7.5 us
    concatenate x2, other arithmetic, grow_blocks(): jnp.concatenate([jnp.where(low, tiles, other), jnp.where(low, other, tile...  6.86 us
  transfers between devices with their start and end apart: 4, of which 3 were waited for; matrix products, arithmetic and copies ran while one was open for 5% of the time, Pallas kernels for 0%

profile of v1, /device:TPU:0, one launch (start us, length us, event | category | flops | bytes accessed | tf_op | source)
XLA Modules:
  0.0 333.8 jit_solution(3769213131975449187)
XLA Ops:
  7.2 0.0 all-gather.2.cloned.1.call-start
  7.2 0.7 dynamic_slice.7
  8.0 0.9 fusion.3
  8.8 0.1 broadcast_bitcast_fusion
  8.9 2.3 broadcast_multiply_fusion
  11.2 0.0 all-gather.2.cloned.1.call-update
  11.2 0.0 reduce-scatter.2.cloned.1.call-start
  11.3 1.9 copy.10
  13.2 0.0 copy-start.2
  13.2 3.1 collective-permute-start
  16.3 0.0 copy-done.2
  16.3 45.7 %collective-permute-done = f32[1,512,1024]{1,2,0:T(8,128)} collective-permute-done((f32[1,512,1024]{1,2,0:T(8,128)S(1)}, f32[1,512,1024]{1,2,0:T(8,128)}, u32[]{:S(2)}, u32[]{:S(2)}) %collective-permute-start) | collective-permute-done | bytes 2097184 | tf_op jit(solution)/shard_map/ppermute | solution.py:19
  62.0 2.8 broadcast_select_fusion.3
  64.8 0.0 copy-start
  64.8 2.7 pad_maximum_fusion.1
  67.5 0.0 copy-done
  67.5 2.8 collective-permute-start.1
  70.2 180.1 %collective-permute-done.1 = f32[2,512,1024]{1,2,0:T(8,128)} collective-permute-done((f32[2,512,1024]{1,2,0:T(8,128)}, f32[2,512,1024]{1,2,0:T(8,128)}, u32[]{:S(2)}, u32[]{:S(2)}) %collective-permute-start.1) | collective-permute-done | bytes 4194336 | tf_op jit(solution)/shard_map/ppermute | solution.py:19
  250.3 4.7 %broadcast_select_fusion.1 = (f32[2,512,1024]{1,2,0:T(8,128)S(1)}, f32[2,512,1024]{1,2,0:T(8,128)S(1)}) fusion(f32[2,512,1024]{1,2,0:T(8,128)} %collective-permute-done.1, pred[]{:T(512)S(6)} %eq.12, f32[1,512,1024]{1,2,0:T(8,128)} %copy-done, f32[1,512,1024]{1,2,0:T(8,128)S(1)} %get-tuple-element.4), kind=kLoop, calls=%fused_computation.4 | loop fusion | flops 3145728 | bytes 16777216 | tf_op jit(solution)/shard_map/jit(_where)/select_n | solution.py:21
  255.1 4.2 %pad_maximum_fusion = f32[4,512,1024]{1,2,0:T(8,128)} fusion(f32[2,512,1024]{1,2,0:T(8,128)S(1)} %get-tuple-element.3, f32[2,512,1024]{1,2,0:T(8,128)S(1)} %get-tuple-element.2), kind=kLoop, calls=%fused_computation | loop fusion | flops 2097152 | bytes 16777216 | tf_op jit(solution)/shard_map/concatenate | solution.py:21
  259.3 0.0 all-gather.2.cloned.1.call-done
  259.3 16.3 %multiply_negate_fusion = f32[512,1024]{1,0:T(8,128)S(1)} fusion(f32[512,4096]{0,1:T(8,128)} %bitcast.21, bf16[4096,1024]{1,0:T(8,128)(2,1)} %all-gather.2.cloned.1.call-done, f32[1024]{0:T(1024)S(1)} %bitcast.26), kind=kOutput, calls=%fused_computation.2 | convolution fusion | flops 25770852352 | bytes 18878464 | tf_op jit(solution)/shard_map/dot_general | solution.py:47
  275.6 0.0 copy-start.3
  275.6 0.0 copy-start.1
  275.6 1.9 copy.14
  277.5 0.1 copy-done.3
  277.6 0.0 copy-done.1
  277.6 3.4 %fusion = f32[2,512,512]{2,1,0:T(8,128)S(1)} fusion(f32[512,2,512]{0,2,1:T(8,128)} %bitcast.23, bf16[64,2,8,512]{3,2,1,0:T(8,128)(2,1)S(1)} %bitcast.20), kind=kOutput, calls=%fused_computation.5 | convolution fusion | flops 3221225472 | bytes 5242880 | tf_op jit(solution)/shard_map/ikc,ikd->ckd/dot_general | solution.py:55
  281.0 0.0 copy-start.4
  281.0 1.9 copy.13
  282.9 0.0 reduce-scatter.2.cloned.1.call-update
  282.9 42.4 %reduce-scatter.2.cloned.1.call-done = f32[64,1024]{1,0:T(8,128)} async-done(((f32[512,1024]{1,0:T(8,128)}), f32[64,1024]{1,0:T(8,128)}) %reduce-scatter.2.cloned.1.call-update) | async-done | bytes 262160 | tf_op jit(solution)/shard_map/reduce_scatter | solution.py:58
  325.3 0.0 copy-done.4
  325.3 1.7 sub.8
  (2 shorter events, 0.0 us)
Async XLA Ops:
  7.2 252.1 %all-gather.2.cloned.1.call-start = ((), (), s32[]{:S(2)}) async-start(), calls=%async_computation.1 | async-start | bytes 9437184 | tf_op jit(solution)/shard_map/all_gather | solution.py:49
  11.2 314.1 %reduce-scatter.2.cloned.1.call-start = ((), (), s32[]{:S(2)}) async-start(), calls=%async_computation.2 | async-start | bytes 2359296 | tf_op jit(solution)/shard_map/reduce_scatter | solution.py:58
  13.2 3.1 copy-start.2
  13.2 48.8 %collective-permute-start = (f32[1,512,1024]{1,2,0:T(8,128)S(1)}, f32[1,512,1024]{1,2,0:T(8,128)}, u32[]{:S(2)}, u32[]{:S(2)}) collective-permute-start(f32[1,512,1024]{1,2,0:T(8,128)S(1)} %bitcast.24), channel_id=1, source_target_pairs={{0,1},{1,0},{2,3},{3,2},{4,5},{5,4},{6,7},{7,6},{8,9},{9,8},{10,11... | collective-permute-start | bytes 6291464 | tf_op jit(solution)/shard_map/ppermute | solution.py:19
  64.8 2.7 copy-start
  67.5 182.9 %collective-permute-start.1 = (f32[2,512,1024]{1,2,0:T(8,128)}, f32[2,512,1024]{1,2,0:T(8,128)}, u32[]{:S(2)}, u32[]{:S(2)}) collective-permute-start(f32[2,512,1024]{1,2,0:T(8,128)} %pad_maximum_fusion.1), channel_id=1, source_target_pairs={{0,2},{1,3},{2,0},{3,1},{4,6},{5,7},{6,4},{7,5},{8,10},{9,11},{10,... | collective-permute-start | bytes 12582920 | tf_op jit(solution)/shard_map/ppermute | solution.py:19
  275.6 2.0 copy-start.3
  275.6 2.0 copy-start.1
  281.0 44.3 %copy-start.4 = (f32[64,1024]{1,0:T(8,128)S(1)}, f32[64,1024]{1,0:T(8,128)}, u32[]{:S(2)}) copy-start(f32[64,1024]{1,0:T(8,128)} %param.7) | copy-start | bytes 786436
Sparse Core Ops, SparseCore 0:
  11.3 57.0 all-gather.1
  283.0 42.2 reduce-scatter.1
